TPU v7x, 512 devices: a whole 4x4x16 slice. The times are simulated.
512 devices in a mesh: expert: 32 (over z, core), tensor: 16 (over y, x).
Axes of the slice: x: 4, y: 4, z: 16, core: 2. Of those that a mesh axis runs over, the one named last changes fastest.
Arguments:
- hidden_in: bfloat16 [4096, 4096], P('expert', 'tensor'), may hold values from -92 to 92
- norm_gain: float32 [4096], P('tensor'), may hold values from 0.5 to 1.5
- expert_ids: int32 [4096, 8], P('expert'), may hold values from 0 to 63, all different within a row; in each aligned block of 128 rows (0 to 127, 128 to 255, ...) at most 24 rows name the same one
- route_weights: float32 [4096, 8], P('expert'), may hold values from 0.05 to 0.5
- w_gate: bfloat16 [64, 1536, 4096], P('expert', 'tensor'), may hold values from -0.09375 to 0.09375
- w_up: bfloat16 [64, 1536, 4096], P('expert', 'tensor'), may hold values from -0.09375 to 0.09375
- w_down: bfloat16 [64, 1536, 4096], P('expert', 'tensor'), may hold values from -0.15625 to 0.15625
Outputs:
- moe_out: bfloat16 [4096, 4096], P('expert', 'tensor')
Inputs may be any that keep to these rules, and one draw needn't show every extreme that they name: `expert_ids`: in each aligned block of 128 rows (the rows of one index of the expert axis) no expert is named by more than 24 rows, a bound that some block reaches.
All inputs are finite; a program needn't handle non-finite values.
Results may differ from a plain program's by a relative error of at most 0.019.
Values may be sent and summed in bfloat16 or wider, within the bound.
A program may use at most 128 MiB of HBM per device.

v0:
```python
import jax
import jax.numpy as jnp
from jax import lax
from jax.sharding import PartitionSpec as P

D = 4096
epsilon = 1e-06


def body(hidden_in, norm_gain, expert_ids, route_weights, w_gate, w_up, w_down):
    tokens_here = hidden_in.shape[0]
    choices_count = expert_ids.shape[1]
    exp_local = w_gate.shape[0]
    groups = lax.axis_size("expert")
    experts_all = exp_local * groups
    capacity = min(tokens_here, 3 * tokens_here * choices_count // (2 * experts_all))
    widened = hidden_in.astype(jnp.float32)
    squares = lax.psum(jnp.sum(widened * widened, axis=1), "tensor")
    normed = (widened * lax.rsqrt(squares / D + epsilon)[:, None] * norm_gain[None, :]).astype(
        jnp.bfloat16
    )
    routing = jnp.concatenate([expert_ids.astype(jnp.float32), route_weights], axis=1)
    routing = lax.all_gather(routing.T, "expert", axis=0, tiled=False)
    tokens_all = lax.all_gather(normed, "expert", axis=0, tiled=False)
    first = (lax.axis_index("expert") * exp_local).astype(jnp.float32)
    named = (
        routing[:, None, :choices_count, :]
        == first + jnp.arange(exp_local, dtype=jnp.float32)[None, :, None, None]
    )
    chosen = jnp.any(named, axis=2)
    scale = jnp.sum(jnp.where(named, routing[:, None, choices_count:, :], 0.0), axis=2)
    step = jnp.arange(tokens_here, dtype=jnp.int32)
    earlier = (step[:, None] < step[None, :]).astype(jnp.bfloat16)
    position = jnp.einsum(
        "bjs,st->bjt", chosen.astype(jnp.bfloat16), earlier, preferred_element_type=jnp.float32
    )
    slot = jnp.arange(capacity, dtype=jnp.float32)
    select = (
        (position[:, :, None, :] == slot[None, None, :, None]) & chosen[:, :, None, :]
    ).astype(jnp.bfloat16)
    rows = jnp.einsum(
        "bjst,btd->bjsd", select, tokens_all, preferred_element_type=jnp.float32
    ).astype(jnp.bfloat16)
    rows = rows.transpose(1, 0, 2, 3).reshape(exp_local, groups * capacity, -1)
    piece = lax.all_gather(rows, "tensor", axis=2, tiled=True)
    gate_add = jnp.einsum("erd,efd->erf", piece, w_gate, preferred_element_type=jnp.float32)
    up_add = jnp.einsum("erd,efd->erf", piece, w_up, preferred_element_type=jnp.float32)
    inner = (jax.nn.silu(gate_add) * up_add).astype(jnp.bfloat16)
    partials = jnp.einsum("erf,efd->erd", inner, w_down, preferred_element_type=jnp.float32).astype(
        jnp.bfloat16
    )
    summed = lax.psum_scatter(partials, "tensor", scatter_dimension=2, tiled=True)
    summed = summed.reshape(exp_local, groups, capacity, -1)
    back = jnp.einsum("bjst,jbsd->bjtd", select, summed, preferred_element_type=jnp.float32)
    weighted = jnp.sum(back * scale[:, :, :, None], axis=1).astype(jnp.bfloat16)
    return lax.psum_scatter(weighted, "expert", scatter_dimension=0, tiled=False)


def solution(mesh):
    placed = (
        P("expert", "tensor"),
        P("tensor"),
        P("expert", None),
        P("expert", None),
        P("expert", "tensor", None),
        P("expert", "tensor", None),
        P("expert", "tensor", None),
    )
    return jax.shard_map(
        body, mesh=mesh, in_specs=placed, out_specs=P("expert", "tensor"), check_vma=False
    )
```

profile of v0, /device:TPU:18, one launch (start us, length us, event | category | flops | bytes accessed | tf_op | source)
XLA Modules:
  0.0 491.3 jit_solution(8719006843433217021)
XLA Ops:
  6.5 0.0 copy-start
  6.5 0.0 all-gather.7.cloned.1.call-start
  6.5 1.1 fusion.17
  7.6 31.1 %psum.7 = f32[128]{0:T(128)S(1)} all-reduce(f32[128]{0:T(128)S(1)} %fusion.17), channel_id=1, replica_groups=mesh['expert'=32,'tensor'=16] {'tensor'}, use_global_device_ids=true, to_apply=%region_2.0 | all-reduce | flops 128 | bytes 1024 | tf_op jit(solution)/shard_map/psum | solution.py:18
  38.8 1.6 fusion.19
  40.3 0.0 all-gather.7.cloned.1.call-update
  40.3 0.0 all-gather.5.cloned.1.call-start
  40.4 0.7 convert_element_type.31
  41.1 0.7 maximum_bitcast_fusion
  41.8 37.0 %all-gather = f32[512,128]{1,0:T(8,128)S(1)} all-gather(f32[16,128]{1,0:T(8,128)S(1)} %maximum_bitcast_fusion), channel_id=2, replica_groups=mesh['expert'=32,'tensor'=16] {'expert'}, dimensions={0}, use_global_device_ids=true | all-gather | bytes 270336 | tf_op jit(solution)/shard_map/all_gather | solution.py:23
  78.8 0.2 compare_reduce_fusion
  79.0 0.1 fusion.21
  79.2 41.8 %all-gather.7.cloned.1.call-done = bf16[4096,256]{1,0:T(8,128)(2,1)} async-done(((bf16[128,256]{1,0:T(8,128)(2,1)}), bf16[4096,256]{1,0:T(8,128)(2,1)}) %all-gather.7.cloned.1.call-update) | async-done | bytes 2097168 | tf_op jit(solution)/shard_map/all_gather | solution.py:24
  121.0 2.0 fusion
  123.0 1.0 copy.17
  124.0 0.0 all-gather.5.cloned.1.call-update
  124.0 0.0 reduce-scatter.3.cloned.1.call-start
  124.1 110.4 %all-gather.5.cloned.1.call-done = bf16[2,768,4096]{2,1,0:T(8,128)(2,1)} async-done(((bf16[2,768,256]{2,1,0:T(8,128)(2,1)}), bf16[2,768,4096]{2,1,0:T(8,128)(2,1)}) %all-gather.5.cloned.1.call-update) | async-done | bytes 12582928 | tf_op jit(solution)/shard_map/all_gather | solution.py:45
  234.4 9.0 %fusion.26 = f32[2,768,96]{1,2,0:T(8,128)S(1)} fusion(bf16[2,768,4096]{2,1,0:T(8,128)(2,1)} %all-gather.5.cloned.1.call-done, bf16[2,96,4096]{2,1,0:T(8,128)(2,1)} %param.11), kind=kOutput, calls=%fused_computation.36 | convolution fusion | flops 1207959552 | bytes 14745600 | tf_op jit(solution)/shard_map/erd,efd->erf/dot_general | solution.py:46
  243.4 0.0 copy-done
  243.4 15.3 %convolution_convert_fusion = bf16[2,768,4096]{2,1,0:T(8,128)(2,1)} fusion(bf16[2,96,4096]{2,1,0:T(8,128)(2,1)S(1)} %copy-done, bf16[2,768,4096]{2,1,0:T(8,128)(2,1)} %all-gather.5.cloned.1.call-done, bf16[2,96,4096]{2,1,0:T(8,128)(2,1)} %param.12, f32[2,768,96]{1,2,0:T(8,128)S(1)} %fusion.26), kind=kOutput, calls=%fused_computation | convolution fusion | flops 2423095296 | bytes 28901376 | tf_op jit(solution)/shard_map/erf,efd->erd/dot_general | solution.py:49
  258.7 0.0 reduce-scatter.3.cloned.1.call-update
  258.8 0.0 reduce-scatter.5.cloned.1.call-start
  258.8 0.2 fusion.16
  259.0 109.0 %reduce-scatter.3.cloned.1.call-done = bf16[2,768,256]{2,1,0:T(8,128)(2,1)} async-done(((bf16[2,768,4096]{2,1,0:T(8,128)(2,1)}), bf16[2,768,256]{2,1,0:T(8,128)(2,1)}) %reduce-scatter.3.cloned.1.call-update) | async-done | bytes 786448 | tf_op jit(solution)/shard_map/reduce_scatter | solution.py:52
  368.0 5.3 %multiply_reduce_fusion = bf16[32,128,256]{2,1,0:T(8,128)(2,1)} fusion(f32[32,2,128]{2,1,0:T(2,128)S(1)} %fusion.16, bf16[2,32,24,256]{3,2,1,0:T(8,128)(2,1)} %bitcast.25, f32[32,2,128]{2,1,0:T(2,128)S(1)} %copy.16, pred[32,2,128]{2,1,0:T(4,128)(4,1)S(1)} %compare_reduce_fusion), kind=kOutput, calls=%fused_computation.1 | convolution fusion | flops 104202240 | bytes 2957312 | tf_op jit(solution)/shard_map/bjst,jbsd->bjtd/dot_general | solution.py:54
  373.3 0.0 reduce-scatter.5.cloned.1.call-update
  373.3 111.5 %reduce-scatter.5.cloned.1.call-done = bf16[1,128,256]{2,1,0:T(8,128)(2,1)} async-done(((bf16[32,128,256]{2,1,0:T(8,128)(2,1)}), bf16[1,128,256]{2,1,0:T(8,128)(2,1)}) %reduce-scatter.5.cloned.1.call-update) | async-done | bytes 65552 | tf_op jit(solution)/shard_map/reduce_scatter | solution.py:56
  (4 shorter events, 0.1 us)
Async XLA Ops:
  6.5 236.9 %copy-start = (bf16[2,96,4096]{2,1,0:T(8,128)(2,1)S(1)}, bf16[2,96,4096]{2,1,0:T(8,128)(2,1)}, u32[]{:S(2)}) copy-start(bf16[2,96,4096]{2,1,0:T(8,128)(2,1)} %param.13) | copy-start | bytes 4718596
  6.5 114.5 %all-gather.7.cloned.1.call-start = ((), (), s32[]{:S(2)}) async-start(), calls=%async_computation.5 | async-start | bytes 2162688 | tf_op jit(solution)/shard_map/all_gather | solution.py:24
  40.3 194.1 %all-gather.5.cloned.1.call-start = ((), (), s32[]{:S(2)}) async-start(), calls=%async_computation.2 | async-start | bytes 13369344 | tf_op jit(solution)/shard_map/all_gather | solution.py:45
  124.0 243.9 %reduce-scatter.3.cloned.1.call-start = ((), (), s32[]{:S(2)}) async-start(), calls=%async_computation.3 | async-start | bytes 13369344 | tf_op jit(solution)/shard_map/reduce_scatter | solution.py:52
  258.8 226.0 %reduce-scatter.5.cloned.1.call-start = ((), (), s32[]{:S(2)}) async-start(), calls=%async_computation.4 | async-start | bytes 2162688 | tf_op jit(solution)/shard_map/reduce_scatter | solution.py:56
Sparse Core Ops, SparseCore 0:
  40.5 80.4 all-gather.6
  124.1 110.2 all-gather.4
  258.9 109.0 reduce-scatter.2
  373.4 111.3 reduce-scatter.4
where the time goes:
time: 492 us; the launch traced here: 491 us
  waiting for transfers between devices  373 us (76%)
  blocking collectives  68.2 us (14%)
  matrix products  31.7 us (6%)
  between operations  13.2 us (3%)
    reduce_scatter x1, waiting for transfers between devices, body(): lax.psum_scatter(weighted, 'expert', scatter_dimension=0, tiled=False)  111 us
    all_gather x1, waiting for transfers between devices, body(): piece = lax.all_gather(rows, 'tensor', axis=2, tiled=True)  110 us
    reduce_scatter x1, waiting for transfers between devices, body(): lax.psum_scatter(partials, 'tensor', scatter_dimension=2, tiled=True)  109 us
    all_gather x1, waiting for transfers between devices, body(): tokens_all = lax.all_gather(normed, 'expert', axis=0, tiled=False)  41.8 us
    all_gather x1, blocking collectives, body(): routing = lax.all_gather(routing.T, 'expert', axis=0, tiled=False)  37 us
    psum x1, blocking collectives, body(): squares = lax.psum(jnp.sum(widened * widened, axis=1), 'tensor')  31.1 us
    dot_general x1, matrix products, body(): jnp.einsum('erf,efd->erd', inner, w_down, preferred_element_type=jnp.floa...  15.3 us
  transfers between devices with their start and end apart: 4, of which 4 were waited for; matrix products, arithmetic and copies ran while one was open for 0% of the time, Pallas kernels for 0%

commit v1 on v0

--- a/solution.py
+++ b/solution.py
@@ -42,7 +42,9 @@
         "bjst,btd->bjsd", select, tokens_all, preferred_element_type=jnp.float32
     ).astype(jnp.bfloat16)
     rows = rows.transpose(1, 0, 2, 3).reshape(exp_local, groups * capacity, -1)
-    piece = lax.all_gather(rows, "tensor", axis=2, tiled=True)
+    piece = jnp.concatenate(
+        lax.all_to_all(jnp.stack([rows] * lax.axis_size("tensor")), "tensor", 0, 0), axis=2
+    )
     gate_add = jnp.einsum("erd,efd->erf", piece, w_gate, preferred_element_type=jnp.float32)
     up_add = jnp.einsum("erd,efd->erf", piece, w_up, preferred_element_type=jnp.float32)
     inner = (jax.nn.silu(gate_add) * up_add).astype(jnp.bfloat16)

time: 492 us -> 532 us (1.081)
  the two profiles are of different devices: /device:TPU:18 before, /device:TPU:2 now
where the time goes in v1:
time: 532 us
  waiting for transfers between devices  250 us (47%)
  blocking collectives  221 us (42%)
  matrix products  31.8 us (6%)
  between operations  13.2 us (2%)
  local copies, waits for them, and re-layouts  11.5 us (2%)
    all_to_all x1, blocking collectives, body(): lax.all_to_all(jnp.stack([rows] * lax.axis_size('tensor')), 'tensor', 0, 0)  147 us
    reduce_scatter x1, waiting for transfers between devices, body(): lax.psum_scatter(weighted, 'expert', scatter_dimension=0, tiled=False)  110 us
    reduce_scatter x1, waiting for transfers between devices, body(): lax.psum_scatter(partials, 'tensor', scatter_dimension=2, tiled=True)  103 us
    psum x1, blocking collectives, body(): squares = lax.psum(jnp.sum(widened * widened, axis=1), 'tensor')  41.4 us
    all_gather x1, waiting for transfers between devices, body(): tokens_all = lax.all_gather(normed, 'expert', axis=0, tiled=False)  36.6 us
    all_gather x1, blocking collectives, body(): routing = lax.all_gather(routing.T, 'expert', axis=0, tiled=False)  32.2 us
    dot_general x1, matrix products, body(): jnp.einsum('erf,efd->erd', inner, w_down, preferred_element_type=jnp.floa...  15.4 us
  transfers between devices with their start and end apart: 3, of which 3 were waited for; matrix products, arithmetic and copies ran while one was open for 0% of the time, Pallas kernels for 0%

profile of v1, /device:TPU:2, one launch (start us, length us, event | category | flops | bytes accessed | tf_op | source)
XLA Modules:
  0.0 531.6 jit_solution(8178726972316484265)
XLA Ops:
  6.5 0.0 copy-start
  6.5 0.0 all-gather.4.cloned.1.call-start
  6.5 1.1 fusion.17
  7.6 41.4 %psum.7 = f32[128]{0:T(128)S(1)} all-reduce(f32[128]{0:T(128)S(1)} %fusion.17), channel_id=1, replica_groups=mesh['expert'=32,'tensor'=16] {'tensor'}, use_global_device_ids=true, to_apply=%region_2.0 | all-reduce | flops 128 | bytes 1024 | tf_op jit(solution)/shard_map/psum | solution.py:18
  49.0 1.6 fusion.19
  50.5 0.0 all-gather.4.cloned.1.call-update
  50.6 0.0 reduce-scatter.3.cloned.1.call-start
  50.6 0.7 convert_element_type.31
  51.3 0.7 maximum_bitcast_fusion
  52.0 32.2 %all-gather = f32[512,128]{1,0:T(8,128)S(1)} all-gather(f32[16,128]{1,0:T(8,128)S(1)} %maximum_bitcast_fusion), channel_id=2, replica_groups=mesh['expert'=32,'tensor'=16] {'expert'}, dimensions={0}, use_global_device_ids=true | all-gather | bytes 270336 | tf_op jit(solution)/shard_map/all_gather | solution.py:23
  84.3 0.2 compare_reduce_fusion
  84.4 0.1 fusion.21
  84.6 36.6 %all-gather.4.cloned.1.call-done = bf16[4096,256]{1,0:T(8,128)(2,1)} async-done(((bf16[128,256]{1,0:T(8,128)(2,1)}), bf16[4096,256]{1,0:T(8,128)(2,1)}) %all-gather.4.cloned.1.call-update) | async-done | bytes 2097168 | tf_op jit(solution)/shard_map/all_gather | solution.py:24
  121.2 2.0 fusion
  123.2 0.1 copy.22
  123.3 6.0 %stack.3 = bf16[16,2,768,256]{3,2,1,0:T(8,128)(2,1)} broadcast(bf16[2,768,256]{2,1,0:T(8,128)(2,1)S(1)} %bitcast.28), dimensions={1,2,3} | broadcast | bytes 13369344 | tf_op jit(solution)/shard_map/stack | solution.py:46
  129.3 147.0 %all_to_all.5 = bf16[16,2,768,256]{3,2,1,0:T(8,128)(2,1)S(1)} all-to-all(bf16[16,2,768,256]{3,2,1,0:T(8,128)(2,1)} %stack.3), channel_id=1, replica_groups=mesh['expert'=32,'tensor'=16] {'tensor'}, dimensions={0} | all-to-all | bytes 25165824 | tf_op jit(solution)/shard_map/all_to_all | solution.py:46
  276.3 5.4 %copy.26 = bf16[16,2,96,8,256]{4,3,0,2,1:T(8,128)(2,1)} copy(bf16[16,2,96,8,256]{4,3,2,1,0:T(8,128)(2,1)S(1)} %bitcast.27) | data formatting | bytes 25165824 | tf_op jit(solution)/shard_map/reshape | solution.py:45
  281.7 9.0 %fusion.26 = f32[2,768,96]{1,2,0:T(8,128)S(1)} fusion(bf16[2,768,4096]{2,1,0:T(8,128)(2,1)} %bitcast.25, bf16[2,96,4096]{2,1,0:T(8,128)(2,1)} %param.11), kind=kOutput, calls=%fused_computation.36 | convolution fusion | flops 1207959552 | bytes 14745600 | tf_op jit(solution)/shard_map/erd,efd->erf/dot_general | solution.py:48
  290.7 0.0 copy-done
  290.7 15.4 %convolution_convert_fusion = bf16[2,768,4096]{2,1,0:T(8,128)(2,1)} fusion(bf16[2,96,4096]{2,1,0:T(8,128)(2,1)S(1)} %copy-done, bf16[2,768,4096]{2,1,0:T(8,128)(2,1)} %bitcast.26, bf16[2,96,4096]{2,1,0:T(8,128)(2,1)} %param.12, f32[2,768,96]{1,2,0:T(8,128)S(1)} %fusion.26), kind=kOutput, calls=%fused_computation | convolution fusion | flops 2423095296 | bytes 28901376 | tf_op jit(solution)/shard_map/erf,efd->erd/dot_general | solution.py:51
  306.1 0.0 reduce-scatter.3.cloned.1.call-update
  306.1 0.0 reduce-scatter.5.cloned.1.call-start
  306.2 0.2 fusion.16
  306.3 103.4 %reduce-scatter.3.cloned.1.call-done = bf16[2,768,256]{2,1,0:T(8,128)(2,1)} async-done(((bf16[2,768,4096]{2,1,0:T(8,128)(2,1)}), bf16[2,768,256]{2,1,0:T(8,128)(2,1)}) %reduce-scatter.3.cloned.1.call-update) | async-done | bytes 786448 | tf_op jit(solution)/shard_map/reduce_scatter | solution.py:54
  409.7 5.3 multiply_reduce_fusion
  415.0 0.0 reduce-scatter.5.cloned.1.call-update
  415.1 110.0 %reduce-scatter.5.cloned.1.call-done = bf16[1,128,256]{2,1,0:T(8,128)(2,1)} async-done(((bf16[32,128,256]{2,1,0:T(8,128)(2,1)}), bf16[1,128,256]{2,1,0:T(8,128)(2,1)}) %reduce-scatter.5.cloned.1.call-update) | async-done | bytes 65552 | tf_op jit(solution)/shard_map/reduce_scatter | solution.py:58
  (4 shorter events, 0.1 us)
Async XLA Ops:
  6.5 284.2 %copy-start = (bf16[2,96,4096]{2,1,0:T(8,128)(2,1)S(1)}, bf16[2,96,4096]{2,1,0:T(8,128)(2,1)}, u32[]{:S(2)}) copy-start(bf16[2,96,4096]{2,1,0:T(8,128)(2,1)} %param.13) | copy-start | bytes 4718596
  6.5 114.7 %all-gather.4.cloned.1.call-start = ((), (), s32[]{:S(2)}) async-start(), calls=%async_computation.5 | async-start | bytes 2162688 | tf_op jit(solution)/shard_map/all_gather | solution.py:24
  50.6 359.2 %reduce-scatter.3.cloned.1.call-start = ((), (), s32[]{:S(2)}) async-start(), calls=%async_computation.3 | async-start | bytes 13369344 | tf_op jit(solution)/shard_map/reduce_scatter | solution.py:54
  306.1 218.9 %reduce-scatter.5.cloned.1.call-start = ((), (), s32[]{:S(2)}) async-start(), calls=%async_computation.4 | async-start | bytes 2162688 | tf_op jit(solution)/shard_map/reduce_scatter | solution.py:58
Sparse Core Ops, SparseCore 0:
  50.7 70.4 all-gather.3
  306.2 103.4 reduce-scatter.2
  415.2 109.8 reduce-scatter.4
